TPU v7x, 32 devices: a whole 2x2x4 slice. The times are simulated.
32 devices in a mesh: section: 2 (over core), ha: 4 (over z), wa: 4 (over y, x).
Axes of the slice: x: 2, y: 2, z: 4, core: 2. Of those that a mesh axis runs over, the one named last changes fastest.
Arguments:
- queries: bfloat16 [2, 1, 32, 64, 1536], P('section', None, 'ha', 'wa'), may hold values from -85 to 85
- keys: bfloat16 [2, 1, 32, 64, 1536], P('section', None, 'ha', 'wa'), may hold values from -4.5 to 4.5
- values: bfloat16 [2, 1, 32, 64, 1536], P('section', None, 'ha', 'wa'), may hold values from -6 to 6
- cotangent: bfloat16 [2, 1, 32, 64, 1536], P('section', None, 'ha', 'wa'), may hold values from -6 to 6
- upstream: bfloat16 [2, 1, 32, 64, 1536], P('section', None, 'ha', 'wa'), may hold values from -6 to 6
- block_mask: int32 [2, 4, 8, 9], P('section', 'ha', 'wa'), may hold values from 0 to 1, as said below
Outputs:
- grad_queries: bfloat16 [2, 1, 32, 64, 1536], P('section', None, 'ha', 'wa')
- grad_keys: bfloat16 [2, 1, 32, 64, 1536], P('section', None, 'ha', 'wa')
- grad_values: bfloat16 [2, 1, 32, 64, 1536], P('section', None, 'ha', 'wa')
Inputs may be any that keep to these rules, and one draw needn't show every extreme that they name: `block_mask`: entry 4, the tile's own block, is always 1.
All inputs are finite; a program needn't handle non-finite values.
Results may differ from a plain program's by a relative error of at most 0.0068.
Values may be sent and summed in bfloat16 or wider, within the bound.
A program may use at most 64 MiB of HBM per device.

v0:
```python
import jax
import jax.numpy as jnp
from jax import lax
from jax.sharding import PartitionSpec as P

HEADS = 12
HEAD_DIM = 128
TILE = 8


def passed_along(value, axis, steps):
    count = lax.axis_size(axis)
    initial, last = (max(0, -steps), min(count, count - steps))
    return lax.ppermute(value, axis, [(source, source + steps) for source in range(initial, last)])


def extended(value, sides, width):
    for axis, dim in sides:
        size, length = (lax.axis_size(axis), value.shape[dim])
        up = [(i, (i + 1) % size) for i in range(size - 1)]
        down = [(j, i) for i, j in up]
        last = lax.slice_in_dim(value, length - width, length, axis=dim)
        initial = lax.slice_in_dim(value, 0, width, axis=dim)
        before = lax.ppermute(last, axis, up)
        after = lax.ppermute(initial, axis, down)
        value = jnp.concatenate([before, value, after], axis=dim)
    return value


def window_live(mask_table, tile_row, tile_col, grid_height, grid_width):
    box_span = 3 * TILE
    offsets = jnp.arange(box_span, dtype=jnp.int32)
    rows_at = tile_row * TILE - TILE + offsets
    cols_at = tile_col * TILE - TILE + offsets
    part_of = offsets // TILE
    thirds = jnp.arange(3, dtype=jnp.int32)
    part_hot = (part_of[:, None] == thirds[None, :]).astype(jnp.float32)
    grid_mask = mask_table.reshape(3, 3).astype(jnp.float32)
    allowed = jnp.dot(jnp.dot(part_hot, grid_mask), part_hot.T)
    inside_rows = (rows_at >= 0) & (rows_at < grid_height)
    inside_cols = (cols_at >= 0) & (cols_at < grid_width)
    return (allowed > 0.5) & inside_rows[:, None] & inside_cols[None, :]


def body(queries, keys, values, cotangent, upstream, block_mask):
    handed = passed_along(upstream, "section", -1)
    paired = jnp.stack((keys, values), axis=0)
    box_kv = extended(paired, (("ha", 3), ("wa", 4)), TILE)
    grad_out = (cotangent.astype(jnp.float32) + handed.astype(jnp.float32)).astype(jnp.bfloat16)
    frames_n = queries.shape[1]
    chan_count = queries.shape[4]
    own_width = queries.shape[3]
    span_count = own_width // TILE
    box_span = 3 * TILE
    ext_width = own_width + 2 * TILE
    query_count = frames_n * TILE * own_width
    region_rows = frames_n * box_span * ext_width
    grid_height = TILE * lax.axis_size("ha")
    grid_width = own_width * lax.axis_size("wa")
    tile_row = lax.axis_index("ha")
    inv_root = HEAD_DIM ** (-0.5)
    region_live = []
    for tile_at in range(span_count):
        tile_col = lax.axis_index("wa") * span_count + tile_at
        live_cells = window_live(
            block_mask[0, 0, tile_at], tile_row, tile_col, grid_height, grid_width
        )
        placed = jnp.pad(
            live_cells, ((0, 0), (tile_at * TILE, ext_width - box_span - tile_at * TILE))
        )
        region_live.append(placed[None].reshape(region_rows))
    live_table = jnp.stack(region_live, axis=0).astype(jnp.float32)
    col_tile = jnp.arange(own_width, dtype=jnp.int32) // TILE
    query_tile = jnp.broadcast_to(col_tile[None, None, :], (frames_n, TILE, own_width)).reshape(
        query_count
    )
    tile_hot = (query_tile[:, None] == jnp.arange(span_count, dtype=jnp.int32)[None, :]).astype(
        jnp.float32
    )
    live_pairs = jnp.dot(tile_hot, live_table) > 0.5
    query_rows = queries[0].reshape(query_count, HEADS, HEAD_DIM)
    grad_rows = grad_out[0].reshape(query_count, HEADS, HEAD_DIM)
    key_rows = box_kv[0, 0].reshape(region_rows, HEADS, HEAD_DIM)
    value_rows = box_kv[1, 0].reshape(region_rows, HEADS, HEAD_DIM)
    scores = (
        jnp.einsum("qhd,khd->hqk", query_rows, key_rows, preferred_element_type=jnp.float32)
        * inv_root
    )
    scores = jnp.where(live_pairs[None], scores, -jnp.inf)
    row_max = jnp.max(scores, axis=2, keepdims=True)
    weights = jnp.exp(scores - row_max)
    softmax_probs = weights / jnp.sum(weights, axis=2, keepdims=True)
    probs_low = softmax_probs.astype(jnp.bfloat16)
    attended = jnp.einsum("hqk,khd->qhd", probs_low, value_rows, preferred_element_type=jnp.float32)
    deltas = jnp.sum(grad_rows.astype(jnp.float32) * attended, axis=2)
    grad_probs = jnp.einsum(
        "qhd,khd->hqk", grad_rows, value_rows, preferred_element_type=jnp.float32
    )
    grad_scores = (softmax_probs * (grad_probs - deltas.T[:, :, None]) * inv_root).astype(
        jnp.bfloat16
    )
    grad_query = jnp.einsum(
        "hqk,khd->qhd", grad_scores, key_rows, preferred_element_type=jnp.float32
    )
    grad_queries = grad_query.reshape(1, frames_n, TILE, own_width, chan_count).astype(jnp.bfloat16)
    weight_pair = jnp.stack((grad_scores, probs_low), axis=0)
    source_pair = jnp.stack((query_rows, grad_rows), axis=1)
    region_grads = jnp.einsum(
        "shqk,qshd->skhd", weight_pair, source_pair, preferred_element_type=jnp.float32
    )
    region_grads = region_grads.reshape(2, frames_n, box_span, ext_width, chan_count)
    col_send = jnp.concatenate(
        [region_grads[:, :, :, :TILE], region_grads[:, :, :, ext_width - TILE :]], axis=3
    ).astype(jnp.bfloat16)
    col_back = extended(col_send[None], (("wa", 4),), TILE)[0]
    back_width = col_back.shape[3]
    gap_shape = list(col_back.shape)
    gap_shape[3] = own_width - 2 * TILE
    col_gap = jnp.zeros(gap_shape, jnp.float32)
    col_folded = region_grads[:, :, :, TILE : ext_width - TILE] + jnp.concatenate(
        [
            col_back[:, :, :, :TILE].astype(jnp.float32),
            col_gap,
            col_back[:, :, :, back_width - TILE :].astype(jnp.float32),
        ],
        axis=3,
    )
    row_send = jnp.concatenate(
        [col_folded[:, :, :TILE], col_folded[:, :, 2 * TILE :]], axis=2
    ).astype(jnp.bfloat16)
    row_back = extended(row_send[None], (("ha", 3),), TILE)[0]
    folded_all = (
        col_folded[:, :, TILE : 2 * TILE]
        + row_back[:, :, :TILE].astype(jnp.float32)
        + row_back[:, :, 3 * TILE :].astype(jnp.float32)
    ).astype(jnp.bfloat16)
    grad_keys = folded_all[0][None]
    grad_values = folded_all[1][None]
    return (grad_queries, grad_keys, grad_values)


def solution(mesh):
    return jax.shard_map(
        body,
        mesh=mesh,
        in_specs=(
            P("section", None, "ha", "wa", None),
            P("section", None, "ha", "wa", None),
            P("section", None, "ha", "wa", None),
            P("section", None, "ha", "wa", None),
            P("section", None, "ha", "wa", None),
            P("section", "ha", "wa", None),
        ),
        out_specs=(
            P("section", None, "ha", "wa", None),
            P("section", None, "ha", "wa", None),
            P("section", None, "ha", "wa", None),
        ),
        check_vma=False,
    )
```

profile of v0, /device:TPU:0, one launch (start us, length us, event | category | flops | bytes accessed | tf_op | source)
XLA Modules:
  0.0 234.0 jit_solution(6713365596675835233)
XLA Ops:
  3.1 5.6 %collective-permute-start = (bf16[2,1,1,8,16,1536]{5,4,3,2,1,0:T(8,128)(2,1)S(1)}, bf16[2,1,1,8,16,1536]{5,4,3,2,1,0:T(8,128)(2,1)S(1)}, u32[]{:S(2)}, u32[]{:S(2)}) collective-permute-start(bf16[2,1,1,8,16,1536]{5,4,3,2,1,0:T(8,128)(2,1)S(1)} %pad_maximum_fusion.2), channel_id=1, source_target_pairs={{0,4},{4,8},{8,12},{1,5},{5,9},{9,13},{2,6},{6,10},{10,14},{3,7},{... | collective-permute-start | bytes 2359304 | tf_op jit(solution)/shard_map/ppermute | solution.py:24
  8.7 1.3 collective-permute-start.4
  10.9 13.4 %collective-permute-done.1 = bf16[2,1,1,8,16,1536]{5,4,3,2,1,0:T(8,128)(2,1)S(1)} collective-permute-done((bf16[2,1,1,8,16,1536]{5,4,3,2,1,0:T(8,128)(2,1)S(1)}, bf16[2,1,1,8,16,1536]{5,4,3,2,1,0:T(8,128)(2,1)S(1)}, u32[]{:S(2)}, u32[]{:S(2)}) %collective-permute-start.1) | collective-permute-done | bytes 786464 | tf_op jit(solution)/shard_map/ppermute | solution.py:25
  25.5 1.4 pad_maximum_fusion.1
  26.9 1.6 fusion.62
  28.5 4.6 %collective-permute-start.2 = (bf16[2,1,1,24,8,1536]{5,4,3,2,1,0:T(8,128)(2,1)}, bf16[2,1,1,24,8,1536]{5,4,3,2,1,0:T(8,128)(2,1)}, u32[]{:S(2)}, u32[]{:S(2)}) collective-permute-start(bf16[2,1,1,24,8,1536]{5,4,3,2,1,0:T(8,128)(2,1)} %get-tuple-element.21), channel_id=1, source_target_pairs={{0,1},{1,2},{2,3},{4,5},{5,6},{6,7},{8,9},{9,10},{10,11},{12,13},{... | collective-permute-start | bytes 3538952 | tf_op jit(solution)/shard_map/ppermute | solution.py:24
  41.0 2.1 copy.38
  44.2 12.1 %collective-permute-done.2 = bf16[2,1,1,24,8,1536]{5,4,3,2,1,0:T(8,128)(2,1)} collective-permute-done((bf16[2,1,1,24,8,1536]{5,4,3,2,1,0:T(8,128)(2,1)}, bf16[2,1,1,24,8,1536]{5,4,3,2,1,0:T(8,128)(2,1)}, u32[]{:S(2)}, u32[]{:S(2)}) %collective-permute-start.2) | collective-permute-done | bytes 1179680 | tf_op jit(solution)/shard_map/ppermute | solution.py:24
  56.4 27.2 %collective-permute-done.3 = bf16[2,1,1,24,8,1536]{5,4,3,2,1,0:T(8,128)(2,1)} collective-permute-done((bf16[2,1,1,24,8,1536]{5,4,3,2,1,0:T(8,128)(2,1)}, bf16[2,1,1,24,8,1536]{5,4,3,2,1,0:T(8,128)(2,1)}, u32[]{:S(2)}, u32[]{:S(2)}) %collective-permute-start.3) | collective-permute-done | bytes 1179680 | tf_op jit(solution)/shard_map/ppermute | solution.py:25
  83.6 2.8 %pad_maximum_fusion = bf16[2,1,1,24,32,1536]{5,4,3,2,1,0:T(8,128)(2,1)S(1)} fusion(bf16[2,1,1,24,8,1536]{5,4,3,2,1,0:T(8,128)(2,1)} %collective-permute-done.3, bf16[2,1,1,8,16,1536]{5,4,3,2,1,0:T(8,128)(2,1)S(1)} %collective-permute-done.1, bf16[1,1,1,8,16,1536]{5,4,3,2,1,0:T(8,128)(2,1)S(1)} %bitcast.69, bf16[1,1,1,8,16,1536]{5,4,3,2,1,0:T(8,128)(2,1)S(1)} %bitcast.72, ...), kind=kLoop, calls=%fused_computation.2 | loop fusion | flops 28311552 | bytes 9437184 | tf_op jit(solution)/shard_map/concatenate | solution.py:26
  86.4 2.7 %fusion.61 = (bf16[1,1,1,24,32,1536]{5,4,3,2,1,0:T(8,128)(2,1)}, bf16[1,1,1,24,32,1536]{5,4,3,2,1,0:T(8,128)(2,1)}) fusion(bf16[2,1,1,24,32,1536]{5,4,3,2,1,0:T(8,128)(2,1)S(1)} %pad_maximum_fusion), kind=kLoop, calls=%fused_computation.79 | loop fusion | bytes 9437184 | tf_op jit(solution)/shard_map/slice | solution.py:84
  89.1 4.2 %reshape_squeeze.17 = bf16[768,12,128]{2,1,0:T(8,128)(2,1)S(1)} reshape(bf16[1,1,1,24,32,1536]{5,4,3,2,1,0:T(8,128)(2,1)} %get-tuple-element.17) | data formatting | bytes 4718592 | tf_op jit(solution)/shard_map/reshape;squeeze | solution.py:84
  93.3 3.4 %copy.31 = bf16[768,12,128]{0,2,1:T(8,128)(2,1)} copy(bf16[768,12,128]{2,1,0:T(8,128)(2,1)S(1)} %reshape_squeeze.17) | data formatting | bytes 4718592 | tf_op jit(solution)/shard_map/reshape;squeeze | solution.py:84
  96.7 5.4 %reshape_squeeze.14 = bf16[768,12,128]{2,1,0:T(8,128)(2,1)} reshape(bf16[1,1,1,24,32,1536]{5,4,3,2,1,0:T(8,128)(2,1)} %get-tuple-element.18) | data formatting | bytes 4718592 | tf_op jit(solution)/shard_map/reshape;squeeze | solution.py:83
  102.1 3.9 %copy.34 = bf16[768,12,128]{0,2,1:T(8,128)(2,1)S(1)} copy(bf16[768,12,128]{2,1,0:T(8,128)(2,1)} %reshape_squeeze.14) | data formatting | bytes 4718592 | tf_op jit(solution)/shard_map/reshape;squeeze | solution.py:83
  106.9 2.2 fusion.63
  111.7 1.4 multiply_convert_fusion
  113.1 1.4 copy-done
  114.5 4.4 %fusion.6 = f32[2,768,12,128]{1,3,2,0:T(8,128)} fusion(bf16[1,12,128,768]{2,3,1,0:T(8,128)(2,1)S(1)} %fusion.73, bf16[1,12,128,768]{2,3,1,0:T(8,128)(2,1)S(1)} %bitcast.66, bf16[128,1,12,128]{0,3,2,1:T(8,128)(2,1)S(1)} %copy-done.8, bf16[128,1,12,128]{0,3,2,1:T(8,128)(2,1)S(1)} %copy-done.7), kind=kOutput, calls=%fused_computation.12 | convolution fusion | flops 606732288 | bytes 14942208 | tf_op jit(solution)/shard_map/shqk,qshd->skhd/dot_general | solution.py:108
  118.9 12.7 %copy.40 = f32[2,768,12,128]{3,2,1,0:T(8,128)} copy(f32[2,768,12,128]{1,3,2,0:T(8,128)} %fusion.6) | data formatting | bytes 18874368 | tf_op jit(solution)/shard_map/shqk,qshd->skhd/transpose | solution.py:108
  131.5 11.9 %reshape.161 = f32[2,1,24,32,1536]{4,3,2,0,1:T(8,128)} reshape(f32[2,768,12,128]{3,2,1,0:T(8,128)} %copy.40) | data formatting | bytes 18874368 | tf_op jit(solution)/shard_map/reshape | solution.py:111
  143.4 4.6 %convert.17 = bf16[2,1,24,32,1536]{4,3,2,0,1:T(8,128)(2,1)S(1)} convert(f32[2,1,24,32,1536]{4,3,2,0,1:T(8,128)} %reshape.161) | non-fusion elementwise | flops 2359296 | bytes 14155776 | tf_op jit(solution)/shard_map/convert.10
  148.2 3.5 %collective-permute-start.5 = (bf16[1,2,1,24,8,1536]{5,4,3,1,2,0:T(8,128)(2,1)S(1)}, bf16[1,2,1,24,8,1536]{5,4,3,1,2,0:T(8,128)(2,1)S(1)}, u32[]{:S(2)}, u32[]{:S(2)}) collective-permute-start(bf16[1,2,1,24,8,1536]{5,4,3,1,2,0:T(8,128)(2,1)S(1)} %get-tuple-element.15), channel_id=1, source_target_pairs={{0,1},{1,2},{2,3},{4,5},{5,6},{6,7},{8,9},{9,10},{10,11},{12,13},{... | collective-permute-start | bytes 3538952 | tf_op jit(solution)/shard_map/ppermute | solution.py:24
  151.7 1.6 collective-permute-start.6
  153.3 21.5 %collective-permute-done.5 = bf16[1,2,1,24,8,1536]{5,4,3,1,2,0:T(8,128)(2,1)S(1)} collective-permute-done((bf16[1,2,1,24,8,1536]{5,4,3,1,2,0:T(8,128)(2,1)S(1)}, bf16[1,2,1,24,8,1536]{5,4,3,1,2,0:T(8,128)(2,1)S(1)}, u32[]{:S(2)}, u32[]{:S(2)}) %collective-permute-start.5) | collective-permute-done | bytes 1179680 | tf_op jit(solution)/shard_map/ppermute | solution.py:24
  174.7 26.0 %collective-permute-done.6 = bf16[1,2,1,24,8,1536]{5,4,3,1,2,0:T(8,128)(2,1)S(1)} collective-permute-done((bf16[1,2,1,24,8,1536]{5,4,3,1,2,0:T(8,128)(2,1)S(1)}, bf16[1,2,1,24,8,1536]{5,4,3,1,2,0:T(8,128)(2,1)S(1)}, u32[]{:S(2)}, u32[]{:S(2)}) %collective-permute-start.6) | collective-permute-done | bytes 1179680 | tf_op jit(solution)/shard_map/ppermute | solution.py:25
  201.6 3.2 %fusion.59 = (bf16[2,1,24,16,1536]{4,3,2,0,1:T(8,128)(2,1)S(1)}, f32[2,1,24,16,1536]{4,3,2,0,1:T(8,128)}) fusion(bf16[2,1,24,8,1536]{4,3,2,0,1:T(8,128)(2,1)S(1)} %get-tuple-element.14, bf16[2,1,24,8,1536]{4,3,2,0,1:T(8,128)(2,1)S(1)} %get-tuple-element.13, f32[2,1,24,32,1536]{4,3,2,0,1:T(8,128)S(1)} %bitcast.65), kind=kLoop, calls=%fused_computation.77 | loop fusion | flops 7077888 | bytes 14155776 | tf_op jit(solution)/shard_map/convert.4
  205.7 5.3 %collective-permute-start.7 = (bf16[1,2,1,8,16,1536]{5,4,3,1,2,0:T(8,128)(2,1)S(1)}, bf16[1,2,1,8,16,1536]{5,4,3,1,2,0:T(8,128)(2,1)}, u32[]{:S(2)}, u32[]{:S(2)}) collective-permute-start(bf16[1,2,1,8,16,1536]{5,4,3,1,2,0:T(8,128)(2,1)S(1)} %get-tuple-element.19), channel_id=1, source_target_pairs={{0,4},{4,8},{8,12},{1,5},{5,9},{9,13},{2,6},{6,10},{10,14},{3,7},{... | collective-permute-start | bytes 2359304 | tf_op jit(solution)/shard_map/ppermute | solution.py:24
  214.6 9.6 %collective-permute-done.7 = bf16[1,2,1,8,16,1536]{5,4,3,1,2,0:T(8,128)(2,1)} collective-permute-done((bf16[1,2,1,8,16,1536]{5,4,3,1,2,0:T(8,128)(2,1)S(1)}, bf16[1,2,1,8,16,1536]{5,4,3,1,2,0:T(8,128)(2,1)}, u32[]{:S(2)}, u32[]{:S(2)}) %collective-permute-start.7) | collective-permute-done | bytes 786464 | tf_op jit(solution)/shard_map/ppermute | solution.py:24
  224.1 5.3 %collective-permute-done.8 = bf16[1,2,1,8,16,1536]{5,4,3,1,2,0:T(8,128)(2,1)} collective-permute-done((bf16[1,2,1,8,16,1536]{5,4,3,1,2,0:T(8,128)(2,1)}, bf16[1,2,1,8,16,1536]{5,4,3,1,2,0:T(8,128)(2,1)}, u32[]{:S(2)}, u32[]{:S(2)}) %collective-permute-start.8) | collective-permute-done | bytes 786464 | tf_op jit(solution)/shard_map/ppermute | solution.py:25
  229.5 1.8 maximum_bitcast_fusion.1
  231.3 1.8 fusion.14
  (67 shorter events, 23.4 us)
Async XLA Ops:
  1.8 22.5 %collective-permute-start.1 = (bf16[2,1,1,8,16,1536]{5,4,3,2,1,0:T(8,128)(2,1)S(1)}, bf16[2,1,1,8,16,1536]{5,4,3,2,1,0:T(8,128)(2,1)S(1)}, u32[]{:S(2)}, u32[]{:S(2)}) collective-permute-start(bf16[2,1,1,8,16,1536]{5,4,3,2,1,0:T(8,128)(2,1)S(1)} %pad_maximum_fusion.2), channel_id=1, source_target_pairs={{4,0},{8,4},{12,8},{5,1},{9,5},{13,9},{6,2},{10,6},{14,10},{7,3},{... | collective-permute-start | bytes 2359304 | tf_op jit(solution)/shard_map/ppermute | solution.py:25
  3.1 22.3 %collective-permute-start = (bf16[2,1,1,8,16,1536]{5,4,3,2,1,0:T(8,128)(2,1)S(1)}, bf16[2,1,1,8,16,1536]{5,4,3,2,1,0:T(8,128)(2,1)S(1)}, u32[]{:S(2)}, u32[]{:S(2)}) collective-permute-start(bf16[2,1,1,8,16,1536]{5,4,3,2,1,0:T(8,128)(2,1)S(1)} %pad_maximum_fusion.2), channel_id=1, source_target_pairs={{0,4},{4,8},{8,12},{1,5},{5,9},{9,13},{2,6},{6,10},{10,14},{3,7},{... | collective-permute-start | bytes 2359304 | tf_op jit(solution)/shard_map/ppermute | solution.py:24
  8.7 29.7 %collective-permute-start.4 = (bf16[1,1,8,16,1536]{4,3,2,1,0:T(8,128)(2,1)}, bf16[1,1,8,16,1536]{4,3,2,1,0:T(8,128)(2,1)}, u32[]{:S(2)}, u32[]{:S(2)}) collective-permute-start(bf16[1,1,8,16,1536]{4,3,2,1,0:T(8,128)(2,1)} %param.10), channel_id=1, source_target_pairs={{16,0},{17,1},{18,2},{19,3},{20,4},{21,5},{22,6},{23,7},{24,8},{25... | collective-permute-start | bytes 1179656 | tf_op jit(solution)/shard_map/ppermute | solution.py:14
  26.8 8.2 %copy-start.6 = (bf16[1,1,8,16,1536]{4,3,2,1,0:T(8,128)(2,1)S(1)}, bf16[1,1,8,16,1536]{4,3,2,1,0:T(8,128)(2,1)}, u32[]{:S(2)}) copy-start(bf16[1,1,8,16,1536]{4,3,2,1,0:T(8,128)(2,1)} %param.6) | copy-start | bytes 1179652
  28.5 27.9 %collective-permute-start.2 = (bf16[2,1,1,24,8,1536]{5,4,3,2,1,0:T(8,128)(2,1)}, bf16[2,1,1,24,8,1536]{5,4,3,2,1,0:T(8,128)(2,1)}, u32[]{:S(2)}, u32[]{:S(2)}) collective-permute-start(bf16[2,1,1,24,8,1536]{5,4,3,2,1,0:T(8,128)(2,1)} %get-tuple-element.21), channel_id=1, source_target_pairs={{0,1},{1,2},{2,3},{4,5},{5,6},{6,7},{8,9},{9,10},{10,11},{12,13},{... | collective-permute-start | bytes 3538952 | tf_op jit(solution)/shard_map/ppermute | solution.py:24
  33.1 50.5 %collective-permute-start.3 = (bf16[2,1,1,24,8,1536]{5,4,3,2,1,0:T(8,128)(2,1)}, bf16[2,1,1,24,8,1536]{5,4,3,2,1,0:T(8,128)(2,1)}, u32[]{:S(2)}, u32[]{:S(2)}) collective-permute-start(bf16[2,1,1,24,8,1536]{5,4,3,2,1,0:T(8,128)(2,1)} %get-tuple-element.22), channel_id=1, source_target_pairs={{1,0},{2,1},{3,2},{5,4},{6,5},{7,6},{9,8},{10,9},{11,10},{13,12},{... | collective-permute-start | bytes 3538952 | tf_op jit(solution)/shard_map/ppermute | solution.py:25
  37.1 46.5 %copy-start.2 = (bf16[1,1,8,16,1536]{4,3,2,1,0:T(8,128)(2,1)S(1)}, bf16[1,1,8,16,1536]{4,3,2,1,0:T(8,128)(2,1)}, u32[]{:S(2)}) copy-start(bf16[1,1,8,16,1536]{4,3,2,1,0:T(8,128)(2,1)} %param.8) | copy-start | bytes 1179652
  37.1 46.5 %copy-start.3 = (bf16[1,1,8,16,1536]{4,3,2,1,0:T(8,128)(2,1)S(1)}, bf16[1,1,8,16,1536]{4,3,2,1,0:T(8,128)(2,1)}, u32[]{:S(2)}) copy-start(bf16[1,1,8,16,1536]{4,3,2,1,0:T(8,128)(2,1)} %param.7) | copy-start | bytes 1179652
  102.1 3.9 %copy-start.5 = (bf16[128,12,128]{2,1,0:T(8,128)(2,1)S(1)}, bf16[128,12,128]{2,1,0:T(8,128)(2,1)}, u32[]{:S(2)}) copy-start(bf16[128,12,128]{2,1,0:T(8,128)(2,1)} %reshape_squeeze.15) | copy-start | bytes 1179652
  109.0 1.7 copy-start.4
  109.0 1.7 copy-start.9
  111.6 2.9 %copy-start.7 = (bf16[128,1,12,128]{0,3,2,1:T(8,128)(2,1)S(1)}, bf16[128,1,12,128]{0,3,2,1:T(8,128)(2,1)}, u32[]{:S(2)}) copy-start(bf16[128,1,12,128]{0,3,2,1:T(8,128)(2,1)} %copy.37) | copy-start | bytes 1179652
  111.7 2.8 %copy-start.8 = (bf16[128,1,12,128]{0,3,2,1:T(8,128)(2,1)S(1)}, bf16[128,1,12,128]{0,3,2,1:T(8,128)(2,1)}, u32[]{:S(2)}) copy-start(bf16[128,1,12,128]{0,3,2,1:T(8,128)(2,1)} %copy.38) | copy-start | bytes 1179652
  113.1 1.4 copy-start
  143.4 58.1 %slice-start = ((s8[9437184]{0:T(1024)(128)(4,1)}), s8[4194304]{0:T(1024)(128)(4,1)S(1)}, s32[]{:S(2)}) async-start(s8[9437184]{0:T(1024)(128)(4,1)} %bitcast.64), calls=%async_computation | async-start | bytes 8388608
  143.4 58.1 %slice-start.1 = ((s8[9437184]{0:T(1024)(128)(4,1)}), s8[1048576]{0:T(1024)(128)(4,1)S(1)}, s32[]{:S(2)}) async-start(s8[9437184]{0:T(1024)(128)(4,1)} %bitcast.64), calls=%async_computation.1 | async-start | bytes 2097152
  148.2 26.5 %collective-permute-start.5 = (bf16[1,2,1,24,8,1536]{5,4,3,1,2,0:T(8,128)(2,1)S(1)}, bf16[1,2,1,24,8,1536]{5,4,3,1,2,0:T(8,128)(2,1)S(1)}, u32[]{:S(2)}, u32[]{:S(2)}) collective-permute-start(bf16[1,2,1,24,8,1536]{5,4,3,1,2,0:T(8,128)(2,1)S(1)} %get-tuple-element.15), channel_id=1, source_target_pairs={{0,1},{1,2},{2,3},{4,5},{5,6},{6,7},{8,9},{9,10},{10,11},{12,13},{... | collective-permute-start | bytes 3538952 | tf_op jit(solution)/shard_map/ppermute | solution.py:24
  151.7 49.9 %slice-start.2 = ((s8[9437184]{0:T(1024)(128)(4,1)}), s8[4194304]{0:T(1024)(128)(4,1)S(1)}, s32[]{:S(2)}) async-start(s8[9437184]{0:T(1024)(128)(4,1)} %bitcast.64), calls=%async_computation.2 | async-start | bytes 8388608
  151.7 49.0 %collective-permute-start.6 = (bf16[1,2,1,24,8,1536]{5,4,3,1,2,0:T(8,128)(2,1)S(1)}, bf16[1,2,1,24,8,1536]{5,4,3,1,2,0:T(8,128)(2,1)S(1)}, u32[]{:S(2)}, u32[]{:S(2)}) collective-permute-start(bf16[1,2,1,24,8,1536]{5,4,3,1,2,0:T(8,128)(2,1)S(1)} %get-tuple-element.16), channel_id=1, source_target_pairs={{1,0},{2,1},{3,2},{5,4},{6,5},{7,6},{9,8},{10,9},{11,10},{13,12},{... | collective-permute-start | bytes 3538952 | tf_op jit(solution)/shard_map/ppermute | solution.py:25
  204.7 7.6 %copy-start.1 = (bf16[12,128,768]{1,2,0:T(8,128)(2,1)S(1)}, bf16[12,128,768]{1,2,0:T(8,128)(2,1)}, u32[]{:S(2)}) copy-start(bf16[12,128,768]{1,2,0:T(8,128)(2,1)} %copy-done) | copy-start | bytes 7077892
  205.7 18.4 %collective-permute-start.7 = (bf16[1,2,1,8,16,1536]{5,4,3,1,2,0:T(8,128)(2,1)S(1)}, bf16[1,2,1,8,16,1536]{5,4,3,1,2,0:T(8,128)(2,1)}, u32[]{:S(2)}, u32[]{:S(2)}) collective-permute-start(bf16[1,2,1,8,16,1536]{5,4,3,1,2,0:T(8,128)(2,1)S(1)} %get-tuple-element.19), channel_id=1, source_target_pairs={{0,4},{4,8},{8,12},{1,5},{5,9},{9,13},{2,6},{6,10},{10,14},{3,7},{... | collective-permute-start | bytes 2359304 | tf_op jit(solution)/shard_map/ppermute | solution.py:24
  211.0 18.4 %collective-permute-start.8 = (bf16[1,2,1,8,16,1536]{5,4,3,1,2,0:T(8,128)(2,1)}, bf16[1,2,1,8,16,1536]{5,4,3,1,2,0:T(8,128)(2,1)}, u32[]{:S(2)}, u32[]{:S(2)}) collective-permute-start(bf16[1,2,1,8,16,1536]{5,4,3,1,2,0:T(8,128)(2,1)} %get-tuple-element.20), channel_id=1, source_target_pairs={{4,0},{8,4},{12,8},{5,1},{9,5},{13,9},{6,2},{10,6},{14,10},{7,3},{... | collective-permute-start | bytes 2359304 | tf_op jit(solution)/shard_map/ppermute | solution.py:25
where the time goes:
time: 235 us; the launch traced here: 234 us
  waiting for transfers between devices  116 us (49%)
  local copies, waits for them, and re-layouts  60 us (26%)
  starting transfers between devices  25.6 us (11%)
  other arithmetic  21.9 us (9%)
  matrix products  9.17 us (4%)
    ppermute x4, waiting for transfers between devices, extended(): after = lax.ppermute(initial, axis, down)  72 us
    ppermute x4, waiting for transfers between devices, extended(): before = lax.ppermute(last, axis, up)  44.3 us
    ppermute x4, starting transfers between devices, extended(): before = lax.ppermute(last, axis, up)  18.9 us
    transpose x1, local copies, waits for them, and re-layouts, body(): jnp.einsum('shqk,qshd->skhd', weight_pair, source_pair, preferred_element...  12.7 us
    reshape x1, local copies, waits for them, and re-layouts, body(): region_grads.reshape(2, frames_n, box_span, ext_width, chan_count)  11.9 us
    another operation x2, local copies, waits for them, and re-layouts, body(): key_rows = box_kv[0, 0].reshape(region_rows, HEADS, HEAD_DIM)  9.32 us
    another operation x2, other arithmetic  7.72 us
    another operation x2, local copies, waits for them, and re-layouts, body(): value_rows = box_kv[1, 0].reshape(region_rows, HEADS, HEAD_DIM)  7.58 us
  transfers between devices with their start and end apart: 9, of which 8 were waited for; matrix products, arithmetic and copies ran while one was open for 7% of the time, Pallas kernels for 0%

commit v1 on v0

--- a/solution.py
+++ b/solution.py
@@ -1,6 +1,10 @@
+import functools
+
 import jax
 import jax.numpy as jnp
 from jax import lax
+from jax.experimental import pallas as pl
+from jax.experimental.pallas import tpu as pltpu
 from jax.sharding import PartitionSpec as P
 
 HEADS = 12
@@ -139,9 +143,373 @@
     return (grad_queries, grad_keys, grad_values)
 
 
+NEG = -1e30
+LANES = 128
+MESH_ID = pl.DeviceIdType.MESH
+
+
+def to_tiles(block):
+    return jnp.concatenate(
+        [block[r * 16 + t * 8 : r * 16 + t * 8 + 8] for t in range(2) for r in range(8)], axis=0
+    )
+
+
+def from_tiles(block):
+    return jnp.concatenate(
+        [block[t * 64 + r * 8 : t * 64 + r * 8 + 8] for r in range(8) for t in range(2)], axis=0
+    )
+
+
+def fused_kernel(
+    sections, rows_n, cols_n,
+    q_ref, k_ref, v_ref, c_ref, u_ref, mask_ref,
+    oq_ref, ok_ref, ov_ref,
+    handed, kv_send, qg_send, bias_send, kv_buf, qg_buf, bias_buf, acc,
+    dz_send, dz_recv, dq_send, dq_recv, dkv_send, dkv_recv,
+    sec_sem, kv_sem, qg_sem, bias_sem, z_sem, dz_sem, dq_sem, dkv_sem,
+):
+    f32, bf16 = jnp.float32, jnp.bfloat16
+    sec = lax.axis_index("section")
+    row = lax.axis_index("ha")
+    col = lax.axis_index("wa")
+    own_heads = HEADS // cols_n
+    tiles = 2 * cols_n
+    peers = [lax.rem(col + j, cols_n) for j in range(1, cols_n)]
+    has_up, has_down = row > 0, row < rows_n - 1
+    inv_root = HEAD_DIM ** (-0.5)
+    scale = inv_root * 1.4426950408889634
+
+    barrier = pltpu.get_barrier_semaphore()
+    for peer in peers:
+        pl.semaphore_signal(barrier, inc=1, device_id={"wa": peer}, device_id_type=MESH_ID)
+    for cond, dev in (
+        (has_up, {"ha": row - 1}),
+        (has_down, {"ha": row + 1}),
+        (sec > 0, {"section": sec - 1}),
+        (sec < sections - 1, {"section": sec + 1}),
+    ):
+        @pl.when(cond)
+        def _(dev=dev):
+            pl.semaphore_signal(barrier, inc=1, device_id=dev, device_id_type=MESH_ID)
+
+    def remote(src, dst, sems, at, dev):
+        return pltpu.make_async_remote_copy(
+            src_ref=src, dst_ref=dst, send_sem=sems.at[(0, *at)], recv_sem=sems.at[(1, *at)],
+            device_id=dev, device_id_type=MESH_ID,
+        )
+
+    sec_copy = remote(u_ref, handed, sec_sem, (), {"section": sec - 1})
+
+    def kv_copy(h, j):
+        peer = peers[j]
+        return remote(
+            kv_send.at[peer * own_heads + h],
+            kv_buf.at[h, 1, :, pl.ds(1 + 2 * col, 2)],
+            kv_sem, (h, j), {"wa": peer},
+        )
+
+    def qg_copy(h, j):
+        peer = peers[j]
+        return remote(
+            qg_send.at[peer * own_heads + h], qg_buf.at[h, col], qg_sem, (h, j), {"wa": peer}
+        )
+
+    def bias_copy(j):
+        return remote(bias_send, bias_buf.at[col], bias_sem, (j,), {"wa": peers[j]})
+
+    def z_copy(h, d):
+        return remote(
+            kv_buf.at[h, 1, :, pl.ds(1, tiles)],
+            kv_buf.at[h, 2 - 2 * d, :, pl.ds(1, tiles)],
+            z_sem, (h, d), {"ha": row - 1 + 2 * d},
+        )
+
+    def dz_copy(h, d):
+        return remote(
+            dz_send.at[h, d], dz_recv.at[h, d], dz_sem, (h, d), {"ha": row - 1 + 2 * d}
+        )
+
+    def dq_copy(h, j):
+        peer = peers[j]
+        return remote(
+            dq_send.at[h, peer], dq_recv.at[col * own_heads + h], dq_sem, (h, j), {"wa": peer}
+        )
+
+    def dkv_copy(h, j):
+        peer = peers[j]
+        return remote(
+            dkv_send.at[h, peer], dkv_recv.at[col * own_heads + h], dkv_sem, (h, j), {"wa": peer}
+        )
+
+    def head_cols(head):
+        return pl.ds(pl.multiple_of(head * LANES, LANES), LANES)
+
+    total = (
+        cols_n - 1
+        + has_up.astype(jnp.int32) + has_down.astype(jnp.int32)
+        + (sec > 0).astype(jnp.int32) + (sec < sections - 1).astype(jnp.int32)
+    )
+    pl.semaphore_wait(barrier, total)
+
+    @pl.when(sec > 0)
+    def _():
+        sec_copy.start()
+
+    @pl.loop(0, HEADS)
+    def _(head):
+        at = head_cols(head)
+        kv_send[head, 0] = to_tiles(k_ref[:, at].astype(f32)).astype(bf16).reshape(2, 64, LANES)
+        kv_send[head, 1] = to_tiles(v_ref[:, at].astype(f32)).astype(bf16).reshape(2, 64, LANES)
+
+    for h in range(own_heads):
+        for j in range(cols_n - 1):
+            kv_copy(h, j).start()
+
+    lane = lax.broadcasted_iota(jnp.int32, (1, LANES), 1)
+    bias_send[...] = jnp.full(bias_send.shape, NEG, f32)
+    for i in range(3):
+        row_in = (row + (i - 1) >= 0) & (row + (i - 1) < rows_n)
+        for jj in range(4):
+            tile = 2 * col + (jj - 1)
+            inside = row_in & (tile >= 0) & (tile < tiles)
+            first = mask_ref[0, 3 * i + jj] if jj < 3 else jnp.int32(0)
+            second = mask_ref[1, 3 * i + jj - 1] if jj > 0 else jnp.int32(0)
+            seen = jnp.where(lane < 64, first, second) * inside.astype(jnp.int32)
+            bias_send[pl.ds(4 * i + jj, 1), :] = jnp.where(seen > 0, 0.0, NEG).astype(f32)
+    for j in range(cols_n - 1):
+        bias_copy(j).start()
+    bias_buf[col] = bias_send[...]
+
+    zero_tile = jnp.zeros((2, 64, LANES), bf16)
+    for h in range(own_heads):
+        kv_buf[h, 1, :, pl.ds(1 + 2 * col, 2)] = kv_send[col * own_heads + h]
+        for i in range(3):
+            kv_buf[h, i, :, 0] = zero_tile
+            kv_buf[h, i, :, tiles + 1] = zero_tile
+
+    for cond, i in ((row == 0, 0), (row == rows_n - 1, 2)):
+        @pl.when(cond)
+        def _(i=i):
+            for h in range(own_heads):
+                @pl.loop(0, tiles)
+                def _(t, h=h):
+                    kv_buf[h, i, :, t + 1] = zero_tile
+
+    @pl.when(sec == sections - 1)
+    def _():
+        handed[...] = jnp.zeros_like(handed)
+
+    @pl.when(sec < sections - 1)
+    def _():
+        sec_copy.wait_recv()
+
+    @pl.loop(0, HEADS)
+    def _(head):
+        at = head_cols(head)
+        qg_send[head, 0] = to_tiles(q_ref[:, at].astype(f32)).astype(bf16)
+        grad = c_ref[:, at].astype(f32) + handed[:, at].astype(f32)
+        qg_send[head, 1] = to_tiles(grad).astype(bf16)
+
+    for h in range(own_heads):
+        for j in range(cols_n - 1):
+            qg_copy(h, j).start()
+        qg_buf[h, col] = qg_send[col * own_heads + h]
+
+    for h in range(own_heads):
+        for j in range(cols_n - 1):
+            kv_copy(h, j).wait_recv()
+
+        @pl.when(has_up)
+        def _(h=h):
+            z_copy(h, 0).start()
+
+        @pl.when(has_down)
+        def _(h=h):
+            z_copy(h, 1).start()
+
+    for j in range(cols_n - 1):
+        bias_copy(j).wait_recv()
+
+    nt = (((1,), (1,)), ((), ()))
+    tn = (((0,), (0,)), ((), ()))
+
+    def dot(a, b, dims):
+        return lax.dot_general(a, b, dims, preferred_element_type=f32)
+
+    def compute(h):
+        acc[h] = jnp.zeros(acc.shape[1:], f32)
+
+        @pl.loop(0, cols_n)
+        def _(pair):
+            query = qg_buf[h, pair, 0]
+            grad = qg_buf[h, pair, 1]
+            box = pl.ds(2 * pair, 4)
+            key_rows = [kv_buf[h, i, 0, box].reshape(256, LANES) for i in range(3)]
+            value_rows = [kv_buf[h, i, 1, box].reshape(256, LANES) for i in range(3)]
+            blocks = []
+            for i in range(3):
+                part = dot(key_rows[i], query, nt) * scale
+                for jj in range(4):
+                    blocks.append(
+                        part[jj * 64 : jj * 64 + 64] + bias_buf[pair, pl.ds(4 * i + jj, 1), :]
+                    )
+            scores = jnp.concatenate(blocks, axis=0)
+            weights = jnp.exp2(scores - jnp.max(scores, axis=0, keepdims=True))
+            probs = weights * (1.0 / jnp.sum(weights, axis=0, keepdims=True))
+            low = probs.astype(bf16)
+            grad_probs = jnp.concatenate([dot(rows, grad, nt) for rows in value_rows], axis=0)
+            deltas = jnp.sum(low.astype(f32) * grad_probs, axis=0, keepdims=True)
+            grad_scores = (probs * (grad_probs - deltas) * inv_root).astype(bf16)
+            keys_all = jnp.concatenate(key_rows, axis=0)
+            dq_send[h, pair] = dot(grad_scores, keys_all, tn).astype(bf16)
+            grad_key = dot(grad_scores, query, (((1,), (0,)), ((), ())))
+            grad_value = dot(low, grad, (((1,), (0,)), ((), ())))
+            for i in range(3):
+                at = slice(i * 256, i * 256 + 256)
+                acc[h, i, 0, box] += grad_key[at].reshape(4, 64, LANES)
+                acc[h, i, 1, box] += grad_value[at].reshape(4, 64, LANES)
+
+    def finish(h):
+        @pl.when(has_down)
+        def _():
+            dz_copy(h, 0).wait_recv()
+
+        @pl.when(has_up)
+        def _():
+            dz_copy(h, 1).wait_recv()
+
+        for cond, d in ((jnp.logical_not(has_down), 0), (jnp.logical_not(has_up), 1)):
+            @pl.when(cond)
+            def _(d=d):
+                dz_recv[h, d] = jnp.zeros(dz_recv.shape[2:], bf16)
+
+        @pl.loop(0, cols_n)
+        def _(pair):
+            for kv in range(2):
+                total = (
+                    acc[h, 1, kv, pl.ds(1 + 2 * pair, 2)]
+                    + dz_recv[h, 0, kv, pl.ds(2 * pair, 2)].astype(f32)
+                    + dz_recv[h, 1, kv, pl.ds(2 * pair, 2)].astype(f32)
+                )
+                dkv_send[h, pair, kv] = total.astype(bf16).reshape(128, LANES)
+
+        for j in range(cols_n - 1):
+            dkv_copy(h, j).start()
+        dkv_recv[col * own_heads + h] = dkv_send[h, col]
+
+    for h in range(own_heads):
+        for j in range(cols_n - 1):
+            qg_copy(h, j).wait_recv()
+
+        @pl.when(has_down)
+        def _(h=h):
+            z_copy(h, 0).wait_recv()
+
+        @pl.when(has_up)
+        def _(h=h):
+            z_copy(h, 1).wait_recv()
+
+        compute(h)
+        for d, cond in ((0, has_up), (1, has_down)):
+            @pl.when(cond)
+            def _(d=d, h=h):
+                for kv in range(2):
+                    dz_send[h, d, kv] = acc[h, 2 * d, kv, pl.ds(1, tiles)].astype(bf16)
+                dz_copy(h, d).start()
+        for j in range(cols_n - 1):
+            dq_copy(h, j).start()
+        dq_recv[col * own_heads + h] = dq_send[h, col]
+        if h > 0:
+            finish(h - 1)
+    finish(own_heads - 1)
+
+    for h in range(own_heads):
+        for j in range(cols_n - 1):
+            dq_copy(h, j).wait_recv()
+
+    @pl.loop(0, HEADS)
+    def _(head):
+        oq_ref[:, head_cols(head)] = from_tiles(dq_recv[head].astype(f32)).astype(bf16)
+
+    for h in range(own_heads):
+        for j in range(cols_n - 1):
+            dkv_copy(h, j).wait_recv()
+
+    @pl.loop(0, HEADS)
+    def _(head):
+        ok_ref[:, head_cols(head)] = from_tiles(dkv_recv[head, 0].astype(f32)).astype(bf16)
+        ov_ref[:, head_cols(head)] = from_tiles(dkv_recv[head, 1].astype(f32)).astype(bf16)
+
+    @pl.when(sec > 0)
+    def _():
+        sec_copy.wait_send()
+
+    for j in range(cols_n - 1):
+        bias_copy(j).wait_send()
+        for h in range(own_heads):
+            for copy in (kv_copy, qg_copy, dq_copy, dkv_copy):
+                copy(h, j).wait_send()
+    for d, cond in ((0, has_up), (1, has_down)):
+        @pl.when(cond)
+        def _(d=d):
+            for h in range(own_heads):
+                z_copy(h, d).wait_send()
+                dz_copy(h, d).wait_send()
+
+
+def fused_body(queries, keys, values, cotangent, upstream, block_mask):
+    sections, rows_n, cols_n = (lax.axis_size(a) for a in ("section", "ha", "wa"))
+    shape = queries.shape
+    tokens = shape[1] * shape[2] * shape[3]
+    flat = (tokens, shape[4])
+    own = HEADS // cols_n
+    tiles = 2 * cols_n
+    bf16, f32 = jnp.bfloat16, jnp.float32
+    vmem = pl.BlockSpec(memory_space=pltpu.VMEM)
+    dma = pltpu.SemaphoreType.DMA
+    out = pl.pallas_call(
+        functools.partial(fused_kernel, sections, rows_n, cols_n),
+        out_shape=[jax.ShapeDtypeStruct(flat, bf16)] * 3,
+        in_specs=[vmem] * 5 + [pl.BlockSpec(memory_space=pltpu.SMEM)],
+        out_specs=[vmem] * 3,
+        scratch_shapes=[
+            pltpu.VMEM(flat, bf16),
+            pltpu.VMEM((HEADS, 2, 2, 64, LANES), bf16),
+            pltpu.VMEM((HEADS, 2, 128, LANES), bf16),
+            pltpu.VMEM((16, LANES), f32),
+            pltpu.VMEM((own, 3, 2, tiles + 2, 64, LANES), bf16),
+            pltpu.VMEM((own, cols_n, 2, 128, LANES), bf16),
+            pltpu.VMEM((cols_n, 16, LANES), f32),
+            pltpu.VMEM((own, 3, 2, tiles + 2, 64, LANES), f32),
+            pltpu.VMEM((own, 2, 2, tiles, 64, LANES), bf16),
+            pltpu.VMEM((own, 2, 2, tiles, 64, LANES), bf16),
+            pltpu.VMEM((own, cols_n, 128, LANES), bf16),
+            pltpu.VMEM((HEADS, 128, LANES), bf16),
+            pltpu.VMEM((own, cols_n, 2, 128, LANES), bf16),
+            pltpu.VMEM((HEADS, 2, 128, LANES), bf16),
+            dma((2,)),
+            dma((2, own, cols_n - 1)),
+            dma((2, own, cols_n - 1)),
+            dma((2, cols_n - 1)),
+            dma((2, own, 2)),
+            dma((2, own, 2)),
+            dma((2, own, cols_n - 1)),
+            dma((2, own, cols_n - 1)),
+        ],
+        compiler_params=pltpu.CompilerParams(
+            collective_id=0, has_side_effects=True, vmem_limit_bytes=50 * 2**20
+        ),
+    )(
+        queries.reshape(flat), keys.reshape(flat), values.reshape(flat),
+        cotangent.reshape(flat), upstream.reshape(flat), block_mask.reshape(2, 9),
+    )
+    return tuple(x.reshape(shape) for x in out)
+
+
 def solution(mesh):
+    fits = mesh.shape["wa"] == 4
     return jax.shard_map(
-        body,
+        fused_body if fits else body,
         mesh=mesh,
         in_specs=(
             P("section", None, "ha", "wa", None),

time: 235 us -> 59.7 us (0.25)
  waiting for transfers between devices: 116 us -> 0 us
  local copies, waits for them, and re-layouts: 60 us -> 7.89 us
  Pallas kernels: 0 us -> 50.8 us
  starting transfers between devices: 25.6 us -> 0 us
  other arithmetic: 21.9 us -> 0 us
  matrix products: 9.17 us -> 0 us
    ppermute x9 -> x0, waiting for transfers between devices: 116 us -> none  [the longest x4 72 us: extended(): after = lax.ppermute(initial, axis, down)]
    pallas_call x0 -> x1, Pallas kernels: none -> 50.8 us  [fused_body(): pl.pallas_call(functools.partial(fused_kernel, sections, rows_n, cols_n),...]
    ppermute x9 -> x0, starting transfers between devices: 25.6 us -> none  [the longest x4 18.9 us: extended(): before = lax.ppermute(last, axis, up)]
    another operation x13 -> x0, local copies, waits for them, and re-layouts: 24.2 us -> none  [the longest x2 9.32 us: body(): key_rows = box_kv[0, 0].reshape(region_rows, HEADS, HEAD_DIM)]
    transpose x1 -> x0, local copies, waits for them, and re-layouts: 12.7 us -> none  [body(): jnp.einsum('shqk,qshd->skhd', weight_pair, source_pair, preferred_element...]
    reshape x1 -> x0, local copies, waits for them, and re-layouts: 11.9 us -> none  [body(): region_grads.reshape(2, frames_n, box_span, ext_width, chan_count)]
    another operation x4 -> x0, other arithmetic: 9.4 us -> none
    dot_general x8 -> x0, matrix products: 9.17 us -> none  [the longest x1 4.36 us: body(): jnp.einsum('shqk,qshd->skhd', weight_pair, source_pair, preferred_element...]
  transfers between devices with their start and end apart: 9 -> 0, of which waited for: 8 -> 0; matrix products, arithmetic and copies ran while one was open for 7% -> 0% of each run, Pallas kernels for 0% -> 0%
where the time goes in v1:
time: 59.7 us; the launch traced here: 59.4 us
  Pallas kernels  50.8 us (85%)
  local copies, waits for them, and re-layouts  7.89 us (13%)
  between operations  0.65 us (1%)
    pallas_call x1, Pallas kernels, fused_body(): pl.pallas_call(functools.partial(fused_kernel, sections, rows_n, cols_n),...  50.8 us
    unnamed x15, local copies, waits for them, and re-layouts  7.89 us

profile of v1, /device:TPU:0, one launch (start us, length us, event | category | flops | bytes accessed | tf_op | source)
XLA Modules:
  0.0 59.4 jit_solution(17854394638356009543)
XLA Ops:
  0.6 0.0 copy-start.5
  0.6 0.7 %copy-done.5 = s32[1,1,2,9]{3,2,1,0:T(2,128)S(1)} copy-done((s32[1,1,2,9]{3,2,1,0:T(2,128)S(1)}, s32[1,1,2,9]{3,2,1,0:T(2,128)}, u32[]{:S(2)}) %copy-start.5) | copy-done | bytes 96
  1.3 0.0 copy-start
  1.3 1.0 %copy-done = bf16[1,1,8,16,1536]{4,3,2,1,0:T(8,128)(2,1)S(1)} copy-done((bf16[1,1,8,16,1536]{4,3,2,1,0:T(8,128)(2,1)S(1)}, bf16[1,1,8,16,1536]{4,3,2,1,0:T(8,128)(2,1)}, u32[]{:S(2)}) %copy-start) | copy-done | bytes 393240
  2.3 0.0 copy-start.1
  2.3 1.0 %copy-done.1 = bf16[1,1,8,16,1536]{4,3,2,1,0:T(8,128)(2,1)S(1)} copy-done((bf16[1,1,8,16,1536]{4,3,2,1,0:T(8,128)(2,1)S(1)}, bf16[1,1,8,16,1536]{4,3,2,1,0:T(8,128)(2,1)}, u32[]{:S(2)}) %copy-start.1) | copy-done | bytes 393240
  3.3 0.0 copy-start.2
  3.3 1.0 %copy-done.2 = bf16[1,1,8,16,1536]{4,3,2,1,0:T(8,128)(2,1)S(1)} copy-done((bf16[1,1,8,16,1536]{4,3,2,1,0:T(8,128)(2,1)S(1)}, bf16[1,1,8,16,1536]{4,3,2,1,0:T(8,128)(2,1)}, u32[]{:S(2)}) %copy-start.2) | copy-done | bytes 393240
  4.3 0.0 copy-start.3
  4.3 1.0 %copy-done.3 = bf16[1,1,8,16,1536]{4,3,2,1,0:T(8,128)(2,1)S(1)} copy-done((bf16[1,1,8,16,1536]{4,3,2,1,0:T(8,128)(2,1)S(1)}, bf16[1,1,8,16,1536]{4,3,2,1,0:T(8,128)(2,1)}, u32[]{:S(2)}) %copy-start.3) | copy-done | bytes 393240
  5.3 0.0 copy-start.4
  5.3 1.0 %copy-done.4 = bf16[1,1,8,16,1536]{4,3,2,1,0:T(8,128)(2,1)S(1)} copy-done((bf16[1,1,8,16,1536]{4,3,2,1,0:T(8,128)(2,1)S(1)}, bf16[1,1,8,16,1536]{4,3,2,1,0:T(8,128)(2,1)}, u32[]{:S(2)}) %copy-start.4) | copy-done | bytes 393240
  6.3 50.8 %shard_map.85 = (bf16[128,1536]{1,0:T(8,128)(2,1)S(1)}, bf16[128,1536]{1,0:T(8,128)(2,1)S(1)}, bf16[128,1536]{1,0:T(8,128)(2,1)S(1)}) custom-call(bf16[128,1536]{1,0:T(8,128)(2,1)S(1)} %bitcast.9, bf16[128,1536]{1,0:T(8,128)(2,1)S(1)} %bitcast.10, bf16[128,1536]{1,0:T(8,128)(2,1)S(1)} %bitcast.11, bf16[128,1536]{1,0:T(8,128)(2,1)S(1)} %bitcast.12, ...), custom_call_target="tpu_custom_call" | custom-call | tf_op jit(solution)/shard_map/pallas_call | solution.py:470
  57.1 0.7 %copy.12 = bf16[1,1,8,16,1536]{4,3,2,1,0:T(8,128)(2,1)} copy(bf16[1,1,8,16,1536]{4,3,2,1,0:T(8,128)(2,1)S(1)} %bitcast.16) | data formatting | bytes 786432
  57.9 0.7 %copy.13 = bf16[1,1,8,16,1536]{4,3,2,1,0:T(8,128)(2,1)} copy(bf16[1,1,8,16,1536]{4,3,2,1,0:T(8,128)(2,1)S(1)} %bitcast.15) | data formatting | bytes 786432
  58.6 0.7 %copy.14 = bf16[1,1,8,16,1536]{4,3,2,1,0:T(8,128)(2,1)} copy(bf16[1,1,8,16,1536]{4,3,2,1,0:T(8,128)(2,1)S(1)} %bitcast.14) | data formatting | bytes 786432
Async XLA Ops:
  0.6 0.7 %copy-start.5 = (s32[1,1,2,9]{3,2,1,0:T(2,128)S(1)}, s32[1,1,2,9]{3,2,1,0:T(2,128)}, u32[]{:S(2)}) copy-start(s32[1,1,2,9]{3,2,1,0:T(2,128)} %param.11) | copy-start | bytes 220
  1.3 1.0 %copy-start = (bf16[1,1,8,16,1536]{4,3,2,1,0:T(8,128)(2,1)S(1)}, bf16[1,1,8,16,1536]{4,3,2,1,0:T(8,128)(2,1)}, u32[]{:S(2)}) copy-start(bf16[1,1,8,16,1536]{4,3,2,1,0:T(8,128)(2,1)} %param.6) | copy-start | bytes 1179652
  2.3 1.0 %copy-start.1 = (bf16[1,1,8,16,1536]{4,3,2,1,0:T(8,128)(2,1)S(1)}, bf16[1,1,8,16,1536]{4,3,2,1,0:T(8,128)(2,1)}, u32[]{:S(2)}) copy-start(bf16[1,1,8,16,1536]{4,3,2,1,0:T(8,128)(2,1)} %param.7) | copy-start | bytes 1179652
  3.3 1.0 %copy-start.2 = (bf16[1,1,8,16,1536]{4,3,2,1,0:T(8,128)(2,1)S(1)}, bf16[1,1,8,16,1536]{4,3,2,1,0:T(8,128)(2,1)}, u32[]{:S(2)}) copy-start(bf16[1,1,8,16,1536]{4,3,2,1,0:T(8,128)(2,1)} %param.8) | copy-start | bytes 1179652
  4.3 1.0 %copy-start.3 = (bf16[1,1,8,16,1536]{4,3,2,1,0:T(8,128)(2,1)S(1)}, bf16[1,1,8,16,1536]{4,3,2,1,0:T(8,128)(2,1)}, u32[]{:S(2)}) copy-start(bf16[1,1,8,16,1536]{4,3,2,1,0:T(8,128)(2,1)} %param.9) | copy-start | bytes 1179652
  5.3 1.0 %copy-start.4 = (bf16[1,1,8,16,1536]{4,3,2,1,0:T(8,128)(2,1)S(1)}, bf16[1,1,8,16,1536]{4,3,2,1,0:T(8,128)(2,1)}, u32[]{:S(2)}) copy-start(bf16[1,1,8,16,1536]{4,3,2,1,0:T(8,128)(2,1)} %param.10) | copy-start | bytes 1179652

commit v2 on v1

--- a/solution.py
+++ b/solution.py
@@ -162,10 +162,11 @@
 
 def fused_kernel(
     sections, rows_n, cols_n,
-    q_ref, k_ref, v_ref, c_ref, u_ref, mask_ref,
+    q_hbm, k_hbm, v_hbm, c_hbm, u_ref, mask_hbm,
     oq_ref, ok_ref, ov_ref,
     handed, kv_send, qg_send, bias_send, kv_buf, qg_buf, bias_buf, acc,
     dz_send, dz_recv, dq_send, dq_recv, dkv_send, dkv_recv,
+    q_ref, k_ref, v_ref, c_ref, mask_ref, load_sem,
     sec_sem, kv_sem, qg_sem, bias_sem, z_sem, dz_sem, dq_sem, dkv_sem,
 ):
     f32, bf16 = jnp.float32, jnp.bfloat16
@@ -179,6 +180,15 @@
     inv_root = HEAD_DIM ** (-0.5)
     scale = inv_root * 1.4426950408889634
 
+    loads = [
+        pltpu.make_async_copy(src, dst, load_sem.at[n])
+        for n, (src, dst) in enumerate(
+            ((k_hbm, k_ref), (v_hbm, v_ref), (c_hbm, c_ref), (q_hbm, q_ref), (mask_hbm, mask_ref))
+        )
+    ]
+    for load in loads:
+        load.start()
+
     barrier = pltpu.get_barrier_semaphore()
     for peer in peers:
         pl.semaphore_signal(barrier, inc=1, device_id={"wa": peer}, device_id_type=MESH_ID)
@@ -217,12 +227,22 @@
     def bias_copy(j):
         return remote(bias_send, bias_buf.at[col], bias_sem, (j,), {"wa": peers[j]})
 
-    def z_copy(h, d):
+    def z_copy(h, j, d):
+        piece = pl.ds(1 + 2 * lax.rem(col + cols_n - j, cols_n), 2)
         return remote(
-            kv_buf.at[h, 1, :, pl.ds(1, tiles)],
-            kv_buf.at[h, 2 - 2 * d, :, pl.ds(1, tiles)],
-            z_sem, (h, d), {"ha": row - 1 + 2 * d},
-        )
+            kv_buf.at[h, 1, :, piece],
+            kv_buf.at[h, 2 - 2 * d, :, piece],
+            z_sem, (h, j, d), {"ha": row - 1 + 2 * d},
+        )
+
+    def z_start(h, j):
+        @pl.when(has_up)
+        def _():
+            z_copy(h, j, 0).start()
+
+        @pl.when(has_down)
+        def _():
+            z_copy(h, j, 1).start()
 
     def dz_copy(h, d):
         return remote(
@@ -244,6 +264,20 @@
     def head_cols(head):
         return pl.ds(pl.multiple_of(head * LANES, LANES), LANES)
 
+    zero_tile = jnp.zeros((2, 64, LANES), bf16)
+    for h in range(own_heads):
+        for i in range(3):
+            kv_buf[h, i, :, 0] = zero_tile
+            kv_buf[h, i, :, tiles + 1] = zero_tile
+
+    for cond, i in ((row == 0, 0), (row == rows_n - 1, 2)):
+        @pl.when(cond)
+        def _(i=i):
+            for h in range(own_heads):
+                @pl.loop(0, tiles)
+                def _(t, h=h):
+                    kv_buf[h, i, :, t + 1] = zero_tile
+
     total = (
         cols_n - 1
         + has_up.astype(jnp.int32) + has_down.astype(jnp.int32)
@@ -255,16 +289,37 @@
     def _():
         sec_copy.start()
 
-    @pl.loop(0, HEADS)
-    def _(head):
-        at = head_cols(head)
-        kv_send[head, 0] = to_tiles(k_ref[:, at].astype(f32)).astype(bf16).reshape(2, 64, LANES)
-        kv_send[head, 1] = to_tiles(v_ref[:, at].astype(f32)).astype(bf16).reshape(2, 64, LANES)
-
-    for h in range(own_heads):
+    def send_kv(h):
+        @pl.loop(0, cols_n)
+        def _(peer):
+            head = peer * own_heads + h
+            at = head_cols(head)
+            kv_send[head, 0] = to_tiles(k_ref[:, at].astype(f32)).astype(bf16).reshape(2, 64, LANES)
+            kv_send[head, 1] = to_tiles(v_ref[:, at].astype(f32)).astype(bf16).reshape(2, 64, LANES)
+
         for j in range(cols_n - 1):
             kv_copy(h, j).start()
-
+        kv_buf[h, 1, :, pl.ds(1 + 2 * col, 2)] = kv_send[col * own_heads + h]
+        z_start(h, 0)
+
+    def send_qg(h):
+        @pl.loop(0, cols_n)
+        def _(peer):
+            head = peer * own_heads + h
+            at = head_cols(head)
+            qg_send[head, 0] = to_tiles(q_ref[:, at].astype(f32)).astype(bf16)
+            grad = c_ref[:, at].astype(f32) + handed[:, at].astype(f32)
+            qg_send[head, 1] = to_tiles(grad).astype(bf16)
+
+        for j in range(cols_n - 1):
+            qg_copy(h, j).start()
+        qg_buf[h, col] = qg_send[col * own_heads + h]
+
+    loads[0].wait()
+    loads[1].wait()
+    send_kv(0)
+
+    loads[4].wait()
     lane = lax.broadcasted_iota(jnp.int32, (1, LANES), 1)
     bias_send[...] = jnp.full(bias_send.shape, NEG, f32)
     for i in range(3):
@@ -280,21 +335,6 @@
         bias_copy(j).start()
     bias_buf[col] = bias_send[...]
 
-    zero_tile = jnp.zeros((2, 64, LANES), bf16)
-    for h in range(own_heads):
-        kv_buf[h, 1, :, pl.ds(1 + 2 * col, 2)] = kv_send[col * own_heads + h]
-        for i in range(3):
-            kv_buf[h, i, :, 0] = zero_tile
-            kv_buf[h, i, :, tiles + 1] = zero_tile
-
-    for cond, i in ((row == 0, 0), (row == rows_n - 1, 2)):
-        @pl.when(cond)
-        def _(i=i):
-            for h in range(own_heads):
-                @pl.loop(0, tiles)
-                def _(t, h=h):
-                    kv_buf[h, i, :, t + 1] = zero_tile
-
     @pl.when(sec == sections - 1)
     def _():
         handed[...] = jnp.zeros_like(handed)
@@ -303,29 +343,17 @@
     def _():
         sec_copy.wait_recv()
 
-    @pl.loop(0, HEADS)
-    def _(head):
-        at = head_cols(head)
-        qg_send[head, 0] = to_tiles(q_ref[:, at].astype(f32)).astype(bf16)
-        grad = c_ref[:, at].astype(f32) + handed[:, at].astype(f32)
-        qg_send[head, 1] = to_tiles(grad).astype(bf16)
-
-    for h in range(own_heads):
-        for j in range(cols_n - 1):
-            qg_copy(h, j).start()
-        qg_buf[h, col] = qg_send[col * own_heads + h]
-
-    for h in range(own_heads):
-        for j in range(cols_n - 1):
-            kv_copy(h, j).wait_recv()
-
-        @pl.when(has_up)
-        def _(h=h):
-            z_copy(h, 0).start()
-
-        @pl.when(has_down)
-        def _(h=h):
-            z_copy(h, 1).start()
+    loads[2].wait()
+    loads[3].wait()
+    send_qg(0)
+    for h in range(1, own_heads):
+        send_kv(h)
+        send_qg(h)
+
+    def forward(h):
+        for j in range(1, cols_n):
+            kv_copy(h, j - 1).wait_recv()
+            z_start(h, j)
 
     for j in range(cols_n - 1):
         bias_copy(j).wait_recv()
@@ -397,17 +425,22 @@
             dkv_copy(h, j).start()
         dkv_recv[col * own_heads + h] = dkv_send[h, col]
 
+    forward(0)
     for h in range(own_heads):
+        if h + 1 < own_heads:
+            forward(h + 1)
         for j in range(cols_n - 1):
             qg_copy(h, j).wait_recv()
 
         @pl.when(has_down)
         def _(h=h):
-            z_copy(h, 0).wait_recv()
+            for j in range(cols_n):
+                z_copy(h, j, 0).wait_recv()
 
         @pl.when(has_up)
         def _(h=h):
-            z_copy(h, 1).wait_recv()
+            for j in range(cols_n):
+                z_copy(h, j, 1).wait_recv()
 
         compute(h)
         for d, cond in ((0, has_up), (1, has_down)):
@@ -453,7 +486,8 @@
         @pl.when(cond)
         def _(d=d):
             for h in range(own_heads):
-                z_copy(h, d).wait_send()
+                for j in range(cols_n):
+                    z_copy(h, j, d).wait_send()
                 dz_copy(h, d).wait_send()
 
 
@@ -470,7 +504,7 @@
     out = pl.pallas_call(
         functools.partial(fused_kernel, sections, rows_n, cols_n),
         out_shape=[jax.ShapeDtypeStruct(flat, bf16)] * 3,
-        in_specs=[vmem] * 5 + [pl.BlockSpec(memory_space=pltpu.SMEM)],
+        in_specs=[pl.BlockSpec(memory_space=pltpu.HBM)] * 6,
         out_specs=[vmem] * 3,
         scratch_shapes=[
             pltpu.VMEM(flat, bf16),
@@ -487,11 +521,17 @@
             pltpu.VMEM((HEADS, 128, LANES), bf16),
             pltpu.VMEM((own, cols_n, 2, 128, LANES), bf16),
             pltpu.VMEM((HEADS, 2, 128, LANES), bf16),
+            pltpu.VMEM(flat, bf16),
+            pltpu.VMEM(flat, bf16),
+            pltpu.VMEM(flat, bf16),
+            pltpu.VMEM(flat, bf16),
+            pltpu.SMEM((2, 9), jnp.int32),
+            dma((5,)),
             dma((2,)),
             dma((2, own, cols_n - 1)),
             dma((2, own, cols_n - 1)),
             dma((2, cols_n - 1)),
-            dma((2, own, 2)),
+            dma((2, own, cols_n, 2)),
             dma((2, own, 2)),
             dma((2, own, cols_n - 1)),
             dma((2, own, cols_n - 1)),

time: 59.7 us -> 57.7 us (0.966)
  Pallas kernels: 50.8 us -> 48.8 us
    pallas_call x1, Pallas kernels: 50.8 us -> 48.8 us  [fused_body(): pl.pallas_call(functools.partial(fused_kernel, sections, rows_n, cols_n),...]
where the time goes in v2:
time: 57.7 us; the launch traced here: 57.3 us
  Pallas kernels  48.8 us (85%)
  local copies, waits for them, and re-layouts  7.89 us (14%)
  between operations  0.65 us (1%)
    pallas_call x1, Pallas kernels, fused_body(): pl.pallas_call(functools.partial(fused_kernel, sections, rows_n, cols_n),...  48.8 us
    unnamed x15, local copies, waits for them, and re-layouts  7.89 us

profile of v2, /device:TPU:0, one launch (start us, length us, event | category | flops | bytes accessed | tf_op | source)
XLA Modules:
  0.0 57.3 jit_solution(9439307998390778421)
XLA Ops:
  0.6 0.0 copy-start.5
  0.6 0.7 %copy-done.5 = s32[1,1,2,9]{3,2,1,0:T(2,128)S(1)} copy-done((s32[1,1,2,9]{3,2,1,0:T(2,128)S(1)}, s32[1,1,2,9]{3,2,1,0:T(2,128)}, u32[]{:S(2)}) %copy-start.5) | copy-done | bytes 96
  1.3 0.0 copy-start
  1.3 1.0 %copy-done = bf16[1,1,8,16,1536]{4,3,2,1,0:T(8,128)(2,1)S(1)} copy-done((bf16[1,1,8,16,1536]{4,3,2,1,0:T(8,128)(2,1)S(1)}, bf16[1,1,8,16,1536]{4,3,2,1,0:T(8,128)(2,1)}, u32[]{:S(2)}) %copy-start) | copy-done | bytes 393240
  2.3 0.0 copy-start.1
  2.3 1.0 %copy-done.1 = bf16[1,1,8,16,1536]{4,3,2,1,0:T(8,128)(2,1)S(1)} copy-done((bf16[1,1,8,16,1536]{4,3,2,1,0:T(8,128)(2,1)S(1)}, bf16[1,1,8,16,1536]{4,3,2,1,0:T(8,128)(2,1)}, u32[]{:S(2)}) %copy-start.1) | copy-done | bytes 393240
  3.3 0.0 copy-start.2
  3.3 1.0 %copy-done.2 = bf16[1,1,8,16,1536]{4,3,2,1,0:T(8,128)(2,1)S(1)} copy-done((bf16[1,1,8,16,1536]{4,3,2,1,0:T(8,128)(2,1)S(1)}, bf16[1,1,8,16,1536]{4,3,2,1,0:T(8,128)(2,1)}, u32[]{:S(2)}) %copy-start.2) | copy-done | bytes 393240
  4.3 0.0 copy-start.3
  4.3 1.0 %copy-done.3 = bf16[1,1,8,16,1536]{4,3,2,1,0:T(8,128)(2,1)S(1)} copy-done((bf16[1,1,8,16,1536]{4,3,2,1,0:T(8,128)(2,1)S(1)}, bf16[1,1,8,16,1536]{4,3,2,1,0:T(8,128)(2,1)}, u32[]{:S(2)}) %copy-start.3) | copy-done | bytes 393240
  5.3 0.0 copy-start.4
  5.3 1.0 %copy-done.4 = bf16[1,1,8,16,1536]{4,3,2,1,0:T(8,128)(2,1)S(1)} copy-done((bf16[1,1,8,16,1536]{4,3,2,1,0:T(8,128)(2,1)S(1)}, bf16[1,1,8,16,1536]{4,3,2,1,0:T(8,128)(2,1)}, u32[]{:S(2)}) %copy-start.4) | copy-done | bytes 393240
  6.3 48.8 %shard_map.85 = (bf16[128,1536]{1,0:T(8,128)(2,1)S(1)}, bf16[128,1536]{1,0:T(8,128)(2,1)S(1)}, bf16[128,1536]{1,0:T(8,128)(2,1)S(1)}) custom-call(bf16[128,1536]{1,0:T(8,128)(2,1)S(1)} %bitcast.9, bf16[128,1536]{1,0:T(8,128)(2,1)S(1)} %bitcast.10, bf16[128,1536]{1,0:T(8,128)(2,1)S(1)} %bitcast.11, bf16[128,1536]{1,0:T(8,128)(2,1)S(1)} %bitcast.12, ...), custom_call_target="tpu_custom_call" | custom-call | tf_op jit(solution)/shard_map/pallas_call | solution.py:504
  55.1 0.7 %copy.12 = bf16[1,1,8,16,1536]{4,3,2,1,0:T(8,128)(2,1)} copy(bf16[1,1,8,16,1536]{4,3,2,1,0:T(8,128)(2,1)S(1)} %bitcast.16) | data formatting | bytes 786432
  55.8 0.7 %copy.13 = bf16[1,1,8,16,1536]{4,3,2,1,0:T(8,128)(2,1)} copy(bf16[1,1,8,16,1536]{4,3,2,1,0:T(8,128)(2,1)S(1)} %bitcast.15) | data formatting | bytes 786432
  56.6 0.7 %copy.14 = bf16[1,1,8,16,1536]{4,3,2,1,0:T(8,128)(2,1)} copy(bf16[1,1,8,16,1536]{4,3,2,1,0:T(8,128)(2,1)S(1)} %bitcast.14) | data formatting | bytes 786432
Async XLA Ops:
  0.6 0.7 %copy-start.5 = (s32[1,1,2,9]{3,2,1,0:T(2,128)S(1)}, s32[1,1,2,9]{3,2,1,0:T(2,128)}, u32[]{:S(2)}) copy-start(s32[1,1,2,9]{3,2,1,0:T(2,128)} %param.11) | copy-start | bytes 220
  1.3 1.0 %copy-start = (bf16[1,1,8,16,1536]{4,3,2,1,0:T(8,128)(2,1)S(1)}, bf16[1,1,8,16,1536]{4,3,2,1,0:T(8,128)(2,1)}, u32[]{:S(2)}) copy-start(bf16[1,1,8,16,1536]{4,3,2,1,0:T(8,128)(2,1)} %param.6) | copy-start | bytes 1179652
  2.3 1.0 %copy-start.1 = (bf16[1,1,8,16,1536]{4,3,2,1,0:T(8,128)(2,1)S(1)}, bf16[1,1,8,16,1536]{4,3,2,1,0:T(8,128)(2,1)}, u32[]{:S(2)}) copy-start(bf16[1,1,8,16,1536]{4,3,2,1,0:T(8,128)(2,1)} %param.7) | copy-start | bytes 1179652
  3.3 1.0 %copy-start.2 = (bf16[1,1,8,16,1536]{4,3,2,1,0:T(8,128)(2,1)S(1)}, bf16[1,1,8,16,1536]{4,3,2,1,0:T(8,128)(2,1)}, u32[]{:S(2)}) copy-start(bf16[1,1,8,16,1536]{4,3,2,1,0:T(8,128)(2,1)} %param.8) | copy-start | bytes 1179652
  4.3 1.0 %copy-start.3 = (bf16[1,1,8,16,1536]{4,3,2,1,0:T(8,128)(2,1)S(1)}, bf16[1,1,8,16,1536]{4,3,2,1,0:T(8,128)(2,1)}, u32[]{:S(2)}) copy-start(bf16[1,1,8,16,1536]{4,3,2,1,0:T(8,128)(2,1)} %param.9) | copy-start | bytes 1179652
  5.3 1.0 %copy-start.4 = (bf16[1,1,8,16,1536]{4,3,2,1,0:T(8,128)(2,1)S(1)}, bf16[1,1,8,16,1536]{4,3,2,1,0:T(8,128)(2,1)}, u32[]{:S(2)}) copy-start(bf16[1,1,8,16,1536]{4,3,2,1,0:T(8,128)(2,1)} %param.10) | copy-start | bytes 1179652

commit v3 on v2

--- a/solution.py
+++ b/solution.py
@@ -163,10 +163,10 @@
 def fused_kernel(
     sections, rows_n, cols_n,
     q_hbm, k_hbm, v_hbm, c_hbm, u_ref, mask_hbm,
-    oq_ref, ok_ref, ov_ref,
+    oq_hbm, ok_hbm, ov_hbm,
     handed, kv_send, qg_send, bias_send, kv_buf, qg_buf, bias_buf, acc,
     dz_send, dz_recv, dq_send, dq_recv, dkv_send, dkv_recv,
-    q_ref, k_ref, v_ref, c_ref, mask_ref, load_sem,
+    q_ref, k_ref, v_ref, c_ref, mask_ref, load_sem, oq_ref, ok_ref, ov_ref, store_sem,
     sec_sem, kv_sem, qg_sem, bias_sem, z_sem, dz_sem, dq_sem, dkv_sem,
 ):
     f32, bf16 = jnp.float32, jnp.bfloat16
@@ -188,6 +188,10 @@
     ]
     for load in loads:
         load.start()
+    stores = [
+        pltpu.make_async_copy(src, dst, store_sem.at[n])
+        for n, (src, dst) in enumerate(((oq_ref, oq_hbm), (ok_ref, ok_hbm), (ov_ref, ov_hbm)))
+    ]
 
     barrier = pltpu.get_barrier_semaphore()
     for peer in peers:
@@ -454,7 +458,6 @@
         dq_recv[col * own_heads + h] = dq_send[h, col]
         if h > 0:
             finish(h - 1)
-    finish(own_heads - 1)
 
     for h in range(own_heads):
         for j in range(cols_n - 1):
@@ -464,14 +467,25 @@
     def _(head):
         oq_ref[:, head_cols(head)] = from_tiles(dq_recv[head].astype(f32)).astype(bf16)
 
-    for h in range(own_heads):
+    stores[0].start()
+
+    def place(h):
         for j in range(cols_n - 1):
             dkv_copy(h, j).wait_recv()
 
-    @pl.loop(0, HEADS)
-    def _(head):
-        ok_ref[:, head_cols(head)] = from_tiles(dkv_recv[head, 0].astype(f32)).astype(bf16)
-        ov_ref[:, head_cols(head)] = from_tiles(dkv_recv[head, 1].astype(f32)).astype(bf16)
+        @pl.loop(0, cols_n)
+        def _(peer):
+            head = peer * own_heads + h
+            at = head_cols(head)
+            ok_ref[:, at] = from_tiles(dkv_recv[head, 0].astype(f32)).astype(bf16)
+            ov_ref[:, at] = from_tiles(dkv_recv[head, 1].astype(f32)).astype(bf16)
+
+    place(0)
+    finish(own_heads - 1)
+    for h in range(1, own_heads):
+        place(h)
+    stores[1].start()
+    stores[2].start()
 
     @pl.when(sec > 0)
     def _():
@@ -489,6 +503,8 @@
                 for j in range(cols_n):
                     z_copy(h, j, d).wait_send()
                 dz_copy(h, d).wait_send()
+    for store in stores:
+        store.wait()
 
 
 def fused_body(queries, keys, values, cotangent, upstream, block_mask):
@@ -499,13 +515,12 @@
     own = HEADS // cols_n
     tiles = 2 * cols_n
     bf16, f32 = jnp.bfloat16, jnp.float32
-    vmem = pl.BlockSpec(memory_space=pltpu.VMEM)
     dma = pltpu.SemaphoreType.DMA
     out = pl.pallas_call(
         functools.partial(fused_kernel, sections, rows_n, cols_n),
         out_shape=[jax.ShapeDtypeStruct(flat, bf16)] * 3,
         in_specs=[pl.BlockSpec(memory_space=pltpu.HBM)] * 6,
-        out_specs=[vmem] * 3,
+        out_specs=[pl.BlockSpec(memory_space=pltpu.HBM)] * 3,
         scratch_shapes=[
             pltpu.VMEM(flat, bf16),
             pltpu.VMEM((HEADS, 2, 2, 64, LANES), bf16),
@@ -527,6 +542,10 @@
             pltpu.VMEM(flat, bf16),
             pltpu.SMEM((2, 9), jnp.int32),
             dma((5,)),
+            pltpu.VMEM(flat, bf16),
+            pltpu.VMEM(flat, bf16),
+            pltpu.VMEM(flat, bf16),
+            dma((3,)),
             dma((2,)),
             dma((2, own, cols_n - 1)),
             dma((2, own, cols_n - 1)),
@@ -537,7 +556,7 @@
             dma((2, own, cols_n - 1)),
         ],
         compiler_params=pltpu.CompilerParams(
-            collective_id=0, has_side_effects=True, vmem_limit_bytes=50 * 2**20
+            collective_id=0, has_side_effects=True, vmem_limit_bytes=62 * 2**20
         ),
     )(
         queries.reshape(flat), keys.reshape(flat), values.reshape(flat),

time: 57.7 us -> 53.3 us (0.924)
  local copies, waits for them, and re-layouts: 7.89 us -> 3.7 us
    unnamed x15 -> x7, local copies, waits for them, and re-layouts: 7.89 us -> 3.7 us
where the time goes in v3:
time: 53.3 us; the launch traced here: 53.1 us
  Pallas kernels  48.8 us (92%)
  local copies, waits for them, and re-layouts  3.7 us (7%)
  between operations  0.65 us (1%)
    pallas_call x1, Pallas kernels, fused_body(): pl.pallas_call(functools.partial(fused_kernel, sections, rows_n, cols_n),...  48.8 us
    unnamed x7, local copies, waits for them, and re-layouts  3.7 us

profile of v3, /device:TPU:0, one launch (start us, length us, event | category | flops | bytes accessed | tf_op | source)
XLA Modules:
  0.0 53.1 jit_solution(2643267546262591415)
XLA Ops:
  0.6 48.8 %shard_map.85 = (bf16[128,1536]{1,0:T(8,128)(2,1)}, bf16[128,1536]{1,0:T(8,128)(2,1)}, bf16[128,1536]{1,0:T(8,128)(2,1)}) custom-call(bf16[128,1536]{1,0:T(8,128)(2,1)} %bitcast.9, bf16[128,1536]{1,0:T(8,128)(2,1)} %bitcast.10, bf16[128,1536]{1,0:T(8,128)(2,1)} %bitcast.11, bf16[128,1536]{1,0:T(8,128)(2,1)} %bitcast.12, bf16[128,1536]{1,0:T(8,128)(2,1)} %bitcast.13, ...), custom_call_target="tpu_custom_call" | custom-call | tf_op jit(solution)/shard_map/pallas_call | solution.py:519
  49.4 0.0 copy-start.1
  49.4 1.8 %copy.12 = bf16[1,1,8,16,1536]{4,3,2,1,0:T(8,128)(2,1)} copy(bf16[1,1,8,16,1536]{4,3,2,1,0:T(8,128)(2,1)} %bitcast.16) | data formatting | bytes 786432
  51.3 0.0 copy-done.1
  51.3 0.0 copy-start
  51.3 0.7 %copy.13 = bf16[1,1,8,16,1536]{4,3,2,1,0:T(8,128)(2,1)} copy(bf16[1,1,8,16,1536]{4,3,2,1,0:T(8,128)(2,1)S(1)} %bitcast.15) | data formatting | bytes 786432
  52.0 0.4 copy-done
  52.4 0.7 %copy.14 = bf16[1,1,8,16,1536]{4,3,2,1,0:T(8,128)(2,1)} copy(bf16[1,1,8,16,1536]{4,3,2,1,0:T(8,128)(2,1)S(1)} %bitcast.14) | data formatting | bytes 786432
Async XLA Ops:
  49.4 1.8 %copy-start.1 = (bf16[128,1536]{1,0:T(8,128)(2,1)S(1)}, bf16[128,1536]{1,0:T(8,128)(2,1)}, u32[]{:S(2)}) copy-start(bf16[128,1536]{1,0:T(8,128)(2,1)} %get-tuple-element.7) | copy-start | bytes 1179652
  51.3 1.1 %copy-start = (bf16[128,1536]{1,0:T(8,128)(2,1)S(1)}, bf16[128,1536]{1,0:T(8,128)(2,1)}, u32[]{:S(2)}) copy-start(bf16[128,1536]{1,0:T(8,128)(2,1)} %get-tuple-element.8) | copy-start | bytes 1179652

commit v4 on v3

--- a/solution.py
+++ b/solution.py
@@ -248,10 +248,22 @@
         def _():
             z_copy(h, j, 1).start()
 
-    def dz_copy(h, d):
+    def dz_copy(h, pair, d):
+        piece = pl.ds(2 * pair, 2)
         return remote(
-            dz_send.at[h, d], dz_recv.at[h, d], dz_sem, (h, d), {"ha": row - 1 + 2 * d}
-        )
+            dz_send.at[h, d, :, piece], dz_recv.at[h, d, :, piece],
+            dz_sem, (h, pair, d), {"ha": row - 1 + 2 * d},
+        )
+
+    def dz_start(h, pair):
+        for d, cond in ((0, has_up), (1, has_down)):
+            @pl.when(cond)
+            def _(d=d):
+                for kv in range(2):
+                    dz_send[h, d, kv, pl.ds(2 * pair, 2)] = acc[
+                        h, 2 * d, kv, pl.ds(1 + 2 * pair, 2)
+                    ].astype(bf16)
+                dz_copy(h, pair, d).start()
 
     def dq_copy(h, j):
         peer = peers[j]
@@ -260,7 +272,7 @@
         )
 
     def dkv_copy(h, j):
-        peer = peers[j]
+        peer = lax.rem(col + j + 1, cols_n)
         return remote(
             dkv_send.at[h, peer], dkv_recv.at[col * own_heads + h], dkv_sem, (h, j), {"wa": peer}
         )
@@ -281,6 +293,12 @@
                 @pl.loop(0, tiles)
                 def _(t, h=h):
                     kv_buf[h, i, :, t + 1] = zero_tile
+
+    for d, cond in ((0, row == rows_n - 1), (1, row == 0)):
+        @pl.when(cond)
+        def _(d=d):
+            for h in range(own_heads):
+                dz_recv[h, d] = jnp.zeros(dz_recv.shape[2:], bf16)
 
     total = (
         cols_n - 1
@@ -401,22 +419,23 @@
                 acc[h, i, 0, box] += grad_key[at].reshape(4, 64, LANES)
                 acc[h, i, 1, box] += grad_value[at].reshape(4, 64, LANES)
 
+            @pl.when(pair > 0)
+            def _():
+                dz_start(h, pair - 1)
+
+        dz_start(h, cols_n - 1)
+
     def finish(h):
-        @pl.when(has_down)
-        def _():
-            dz_copy(h, 0).wait_recv()
-
-        @pl.when(has_up)
-        def _():
-            dz_copy(h, 1).wait_recv()
-
-        for cond, d in ((jnp.logical_not(has_down), 0), (jnp.logical_not(has_up), 1)):
-            @pl.when(cond)
-            def _(d=d):
-                dz_recv[h, d] = jnp.zeros(dz_recv.shape[2:], bf16)
-
         @pl.loop(0, cols_n)
         def _(pair):
+            @pl.when(has_down)
+            def _():
+                dz_copy(h, pair, 0).wait_recv()
+
+            @pl.when(has_up)
+            def _():
+                dz_copy(h, pair, 1).wait_recv()
+
             for kv in range(2):
                 total = (
                     acc[h, 1, kv, pl.ds(1 + 2 * pair, 2)]
@@ -425,8 +444,10 @@
                 )
                 dkv_send[h, pair, kv] = total.astype(bf16).reshape(128, LANES)
 
-        for j in range(cols_n - 1):
-            dkv_copy(h, j).start()
+            @pl.when(pair != col)
+            def _():
+                dkv_copy(h, lax.rem(pair - col + cols_n - 1, cols_n)).start()
+
         dkv_recv[col * own_heads + h] = dkv_send[h, col]
 
     forward(0)
@@ -447,12 +468,6 @@
                 z_copy(h, j, 1).wait_recv()
 
         compute(h)
-        for d, cond in ((0, has_up), (1, has_down)):
-            @pl.when(cond)
-            def _(d=d, h=h):
-                for kv in range(2):
-                    dz_send[h, d, kv] = acc[h, 2 * d, kv, pl.ds(1, tiles)].astype(bf16)
-                dz_copy(h, d).start()
         for j in range(cols_n - 1):
             dq_copy(h, j).start()
         dq_recv[col * own_heads + h] = dq_send[h, col]
@@ -502,7 +517,7 @@
             for h in range(own_heads):
                 for j in range(cols_n):
                     z_copy(h, j, d).wait_send()
-                dz_copy(h, d).wait_send()
+                    dz_copy(h, j, d).wait_send()
     for store in stores:
         store.wait()
 
@@ -551,7 +566,7 @@
             dma((2, own, cols_n - 1)),
             dma((2, cols_n - 1)),
             dma((2, own, cols_n, 2)),
-            dma((2, own, 2)),
+            dma((2, own, cols_n, 2)),
             dma((2, own, cols_n - 1)),
             dma((2, own, cols_n - 1)),
         ],

time: 53.3 us -> 50.8 us (0.953)
  Pallas kernels: 48.8 us -> 46.3 us
    pallas_call x1, Pallas kernels: 48.8 us -> 46.3 us  [fused_body(): pl.pallas_call(functools.partial(fused_kernel, sections, rows_n, cols_n),...]
where the time goes in v4:
time: 50.8 us; the launch traced here: 50.6 us
  Pallas kernels  46.3 us (91%)
  local copies, waits for them, and re-layouts  3.7 us (7%)
  between operations  0.65 us (1%)
    pallas_call x1, Pallas kernels, fused_body(): pl.pallas_call(functools.partial(fused_kernel, sections, rows_n, cols_n),...  46.3 us
    unnamed x7, local copies, waits for them, and re-layouts  3.7 us

profile of v4, /device:TPU:0, one launch (start us, length us, event | category | flops | bytes accessed | tf_op | source)
XLA Modules:
  0.0 50.6 jit_solution(15078066888363434075)
XLA Ops:
  0.6 46.3 %shard_map.85 = (bf16[128,1536]{1,0:T(8,128)(2,1)}, bf16[128,1536]{1,0:T(8,128)(2,1)}, bf16[128,1536]{1,0:T(8,128)(2,1)}) custom-call(bf16[128,1536]{1,0:T(8,128)(2,1)} %bitcast.9, bf16[128,1536]{1,0:T(8,128)(2,1)} %bitcast.10, bf16[128,1536]{1,0:T(8,128)(2,1)} %bitcast.11, bf16[128,1536]{1,0:T(8,128)(2,1)} %bitcast.12, bf16[128,1536]{1,0:T(8,128)(2,1)} %bitcast.13, ...), custom_call_target="tpu_custom_call" | custom-call | tf_op jit(solution)/shard_map/pallas_call | solution.py:534
  46.9 0.0 copy-start.1
  46.9 1.8 %copy.12 = bf16[1,1,8,16,1536]{4,3,2,1,0:T(8,128)(2,1)} copy(bf16[1,1,8,16,1536]{4,3,2,1,0:T(8,128)(2,1)} %bitcast.16) | data formatting | bytes 786432
  48.7 0.0 copy-done.1
  48.7 0.0 copy-start
  48.7 0.7 %copy.13 = bf16[1,1,8,16,1536]{4,3,2,1,0:T(8,128)(2,1)} copy(bf16[1,1,8,16,1536]{4,3,2,1,0:T(8,128)(2,1)S(1)} %bitcast.15) | data formatting | bytes 786432
  49.5 0.4 copy-done
  49.9 0.7 %copy.14 = bf16[1,1,8,16,1536]{4,3,2,1,0:T(8,128)(2,1)} copy(bf16[1,1,8,16,1536]{4,3,2,1,0:T(8,128)(2,1)S(1)} %bitcast.14) | data formatting | bytes 786432
Async XLA Ops:
  46.9 1.8 %copy-start.1 = (bf16[128,1536]{1,0:T(8,128)(2,1)S(1)}, bf16[128,1536]{1,0:T(8,128)(2,1)}, u32[]{:S(2)}) copy-start(bf16[128,1536]{1,0:T(8,128)(2,1)} %get-tuple-element.7) | copy-start | bytes 1179652
  48.7 1.1 %copy-start = (bf16[128,1536]{1,0:T(8,128)(2,1)S(1)}, bf16[128,1536]{1,0:T(8,128)(2,1)}, u32[]{:S(2)}) copy-start(bf16[128,1536]{1,0:T(8,128)(2,1)} %get-tuple-element.8) | copy-start | bytes 1179652

commit v5 on v4

--- a/solution.py
+++ b/solution.py
@@ -300,6 +300,9 @@
             for h in range(own_heads):
                 dz_recv[h, d] = jnp.zeros(dz_recv.shape[2:], bf16)
 
+    for h in range(own_heads):
+        acc[h] = jnp.zeros(acc.shape[1:], f32)
+
     total = (
         cols_n - 1
         + has_up.astype(jnp.int32) + has_down.astype(jnp.int32)
@@ -387,8 +390,6 @@
         return lax.dot_general(a, b, dims, preferred_element_type=f32)
 
     def compute(h):
-        acc[h] = jnp.zeros(acc.shape[1:], f32)
-
         @pl.loop(0, cols_n)
         def _(pair):
             query = qg_buf[h, pair, 0]
@@ -473,6 +474,7 @@
         dq_recv[col * own_heads + h] = dq_send[h, col]
         if h > 0:
             finish(h - 1)
+    finish(own_heads - 1)
 
     for h in range(own_heads):
         for j in range(cols_n - 1):
@@ -495,9 +497,7 @@
             ok_ref[:, at] = from_tiles(dkv_recv[head, 0].astype(f32)).astype(bf16)
             ov_ref[:, at] = from_tiles(dkv_recv[head, 1].astype(f32)).astype(bf16)
 
-    place(0)
-    finish(own_heads - 1)
-    for h in range(1, own_heads):
+    for h in range(own_heads):
         place(h)
     stores[1].start()
     stores[2].start()

time: 50.8 us -> 49.5 us (0.974)
  Pallas kernels: 46.3 us -> 44.9 us
    pallas_call x1, Pallas kernels: 46.3 us -> 44.9 us  [fused_body(): pl.pallas_call(functools.partial(fused_kernel, sections, rows_n, cols_n),...]
where the time goes in v5:
time: 49.5 us; the launch traced here: 49.3 us
  Pallas kernels  44.9 us (91%)
  local copies, waits for them, and re-layouts  3.7 us (7%)
  between operations  0.65 us (1%)
    pallas_call x1, Pallas kernels, fused_body(): pl.pallas_call(functools.partial(fused_kernel, sections, rows_n, cols_n),...  44.9 us
    unnamed x7, local copies, waits for them, and re-layouts  3.7 us

profile of v5, /device:TPU:0, one launch (start us, length us, event | category | flops | bytes accessed | tf_op | source)
XLA Modules:
  0.0 49.3 jit_solution(8428436154127923068)
XLA Ops:
  0.6 44.9 %shard_map.85 = (bf16[128,1536]{1,0:T(8,128)(2,1)}, bf16[128,1536]{1,0:T(8,128)(2,1)}, bf16[128,1536]{1,0:T(8,128)(2,1)}) custom-call(bf16[128,1536]{1,0:T(8,128)(2,1)} %bitcast.9, bf16[128,1536]{1,0:T(8,128)(2,1)} %bitcast.10, bf16[128,1536]{1,0:T(8,128)(2,1)} %bitcast.11, bf16[128,1536]{1,0:T(8,128)(2,1)} %bitcast.12, bf16[128,1536]{1,0:T(8,128)(2,1)} %bitcast.13, ...), custom_call_target="tpu_custom_call" | custom-call | tf_op jit(solution)/shard_map/pallas_call | solution.py:534
  45.6 0.0 copy-start.1
  45.6 1.8 %copy.12 = bf16[1,1,8,16,1536]{4,3,2,1,0:T(8,128)(2,1)} copy(bf16[1,1,8,16,1536]{4,3,2,1,0:T(8,128)(2,1)} %bitcast.16) | data formatting | bytes 786432
  47.4 0.0 copy-done.1
  47.4 0.0 copy-start
  47.4 0.7 %copy.13 = bf16[1,1,8,16,1536]{4,3,2,1,0:T(8,128)(2,1)} copy(bf16[1,1,8,16,1536]{4,3,2,1,0:T(8,128)(2,1)S(1)} %bitcast.15) | data formatting | bytes 786432
  48.1 0.4 copy-done
  48.5 0.7 %copy.14 = bf16[1,1,8,16,1536]{4,3,2,1,0:T(8,128)(2,1)} copy(bf16[1,1,8,16,1536]{4,3,2,1,0:T(8,128)(2,1)S(1)} %bitcast.14) | data formatting | bytes 786432
Async XLA Ops:
  45.6 1.8 %copy-start.1 = (bf16[128,1536]{1,0:T(8,128)(2,1)S(1)}, bf16[128,1536]{1,0:T(8,128)(2,1)}, u32[]{:S(2)}) copy-start(bf16[128,1536]{1,0:T(8,128)(2,1)} %get-tuple-element.7) | copy-start | bytes 1179652
  47.4 1.1 %copy-start = (bf16[128,1536]{1,0:T(8,128)(2,1)S(1)}, bf16[128,1536]{1,0:T(8,128)(2,1)}, u32[]{:S(2)}) copy-start(bf16[128,1536]{1,0:T(8,128)(2,1)} %get-tuple-element.8) | copy-start | bytes 1179652
